TPU v7x, 256 devices: a whole 4x4x8 slice. The times are simulated.
256 devices in a mesh: kv: 8 (over x, core), seq: 8 (over z), vocab: 4 (over y).
Axes of the slice: x: 4, y: 4, z: 8, core: 2. Of those that a mesh axis runs over, the one named last changes fastest.
Arguments:
- hidden_state: bfloat16 [48, 4, 3584], P('kv', 'vocab', 'seq'), may hold values from -6 to 6
- input_projection: bfloat16 [3584, 8, 1024], P('seq', 'kv'), may hold values from -0.09375 to 0.09375
- output_projection: bfloat16 [8, 512, 3584], P('kv', None, 'seq'), may hold values from -0.09375 to 0.09375
- norm_pre_attention: float32 [3584], P('seq'), may hold values from 0.1 to 1.9
- norm_post_attention: float32 [3584], P('seq'), may hold values from 0.1 to 1.9
- norm_pre_feedforward: float32 [3584], P('seq'), may hold values from 0.1 to 1.9
- norm_post_feedforward: float32 [3584], P('seq'), may hold values from 0.1 to 1.9
- norm_final: float32 [3584], P('seq'), may hold values from 0.1 to 1.9
- cache_keys: bfloat16 [4, 16384, 8, 256], P('vocab', 'seq', 'kv')
- cache_values: bfloat16 [4, 16384, 8, 256], P('vocab', 'seq', 'kv')
- cache_length: int32 [4], P('vocab'), may hold values from 1 to 16379, as said below
- ancestors: int32 [4, 48, 48], P('vocab'), may hold values from 0 to 1, as said below
- accepted_path: int32 [4, 5], P('vocab'), may hold values from 0 to 47, as said below
- gate_up_weight: bfloat16 [3584, 2, 14336], P('seq', None, ('kv', 'vocab')), may hold values from -0.09375 to 0.09375
- down_weight: bfloat16 [14336, 3584], P(('kv', 'vocab'), 'seq'), may hold values from -0.046875 to 0.046875
- draft_weight: bfloat16 [4, 3584, 3584], P(None, 'seq', ('kv', 'vocab')), may hold values from -0.09375 to 0.09375
- draft_bias: float32 [4, 3584], P(None, ('kv', 'vocab')), may hold values from -3 to 3
- vocab_weight: bfloat16 [131072, 3584], P(('kv', 'seq', 'vocab'))
- candidate_tokens: int32 [5, 48, 4, 8], replicated, may hold values from 0 to 131071
Outputs:
- keys_updated: bfloat16 [4, 16384, 8, 256], P('vocab', 'seq', 'kv')
- values_updated: bfloat16 [4, 16384, 8, 256], P('vocab', 'seq', 'kv')
- log_normalizer: float32 [5, 48, 4], replicated
- candidate_logits: float32 [5, 48, 4, 8], replicated
Inputs may be any that keep to these rules, and one draw needn't show every extreme that they name: The first cache_length[k] slots of tenant k's cache are filled; in every draw some tenant holds exactly 16379. ancestors[k, t, u] is 1 exactly when u is t or an ancestor of t in tenant k's tree; node 0 is the root and every parent has a lower index than its child. accepted_path[k] lists 5 nodes of tenant k's tree from the root down, each the parent of the next; the last of them is node 47.
All inputs are finite; a program needn't handle non-finite values.
Results may differ from a plain program's by a relative error of at most 0.02.
Values may be sent and summed in bfloat16 or wider, within the bound.
A program may use at most 64 MiB of HBM per device.

v0:
```python
import jax
import jax.numpy as jnp
from jax import lax
from jax.sharding import PartitionSpec as P

MODEL_WIDTH = 3584
HEAD_SIZE = 256
CAND = 8
EPSILON = 1e-06
SCORE_CAP = 50.0
LOGIT_CAP = 30.0


def apply_rotary(vectors, token_positions):
    half_dim = vectors.shape[-1] // 2
    frequency = 10000.0 ** (-2.0 * jnp.arange(half_dim, dtype=jnp.float32) / vectors.shape[-1])
    angles = token_positions.astype(jnp.float32)[..., None] * frequency
    cosine = jnp.cos(angles)
    sine_part = jnp.sin(angles)
    first_half = vectors[..., :half_dim]
    second_half = vectors[..., half_dim:]
    return jnp.concatenate(
        [
            first_half * cosine - second_half * sine_part,
            second_half * cosine + first_half * sine_part,
        ],
        axis=-1,
    )


def capped_weight(scores):
    return jnp.exp(SCORE_CAP * jnp.tanh(scores * 0.0625 / SCORE_CAP))


def row_inverse(values):
    totals = lax.psum(jnp.sum(values * values, axis=-1), "seq")
    return lax.rsqrt(totals / MODEL_WIDTH + EPSILON)[:, None]


def gated_units(gate_up, squares):
    inverse = lax.rsqrt(squares / MODEL_WIDTH + EPSILON)[:, None]
    return (
        jax.nn.gelu(gate_up[:, 0] * inverse, approximate=True) * (gate_up[:, 1] * inverse)
    ).astype(jnp.bfloat16)


def local(
    hidden_state,
    input_projection,
    output_projection,
    norm_pre_attention,
    norm_post_attention,
    norm_pre_feedforward,
    norm_post_feedforward,
    norm_final,
    cache_keys,
    cache_values,
    cache_length,
    ancestors,
    accepted_path,
    gate_up_weight,
    down_weight,
    draft_weight,
    draft_bias,
    vocab_weight,
    candidate_tokens,
):
    tok_block = hidden_state.shape[0]
    kv_count = lax.axis_size("kv")
    tenants = lax.axis_size("vocab")
    tree_size = tok_block * kv_count
    own_state = hidden_state[:, 0, :]
    tenant_state = lax.all_gather(own_state, "kv", axis=0, tiled=True)
    tenant_float = tenant_state.astype(jnp.float32)
    scaled_input = (tenant_float * norm_pre_attention).astype(jnp.bfloat16)
    projected_rows = jnp.einsum(
        "td,dhc->thc", scaled_input, input_projection, preferred_element_type=jnp.float32
    )
    projected_rows, squares = lax.psum(
        (projected_rows, jnp.sum(tenant_float * tenant_float, axis=-1)), "seq"
    )
    projected_rows = projected_rows * lax.rsqrt(squares / MODEL_WIDTH + EPSILON)[:, None, None]
    head_count = projected_rows.shape[1]
    depths = jnp.sum(ancestors[0], axis=-1) - 1
    length = cache_length[0]
    token_positions = length + depths
    query_rows = apply_rotary(
        projected_rows[:, :, : 2 * HEAD_SIZE].reshape(tree_size, head_count, 2, HEAD_SIZE),
        token_positions[:, None, None],
    ).astype(jnp.bfloat16)
    new_keys = apply_rotary(
        projected_rows[:, :, 2 * HEAD_SIZE : 3 * HEAD_SIZE], token_positions[:, None]
    ).astype(jnp.bfloat16)
    new_values = projected_rows[:, :, 3 * HEAD_SIZE :].astype(jnp.bfloat16)
    block_size = cache_keys.shape[1]
    block_start = lax.axis_index("seq") * block_size
    cache_cells = block_start + jnp.arange(block_size, dtype=jnp.int32)
    scores = jnp.einsum(
        "thgc,shc->thgs", query_rows, cache_keys[0], preferred_element_type=jnp.float32
    )
    weights = jnp.where((cache_cells < length)[None, None, None, :], capped_weight(scores), 0.0)
    numerator = jnp.einsum(
        "thgs,shc->thgc",
        weights.astype(jnp.bfloat16),
        cache_values[0],
        preferred_element_type=jnp.float32,
    )
    numerator, denominator = lax.psum((numerator, jnp.sum(weights, axis=-1)), "seq")
    tree_scores = jnp.einsum(
        "thgc,uhc->thgu", query_rows, new_keys, preferred_element_type=jnp.float32
    )
    tree_weights = jnp.where(ancestors[0][:, None, None, :] > 0, capped_weight(tree_scores), 0.0)
    numerator = numerator + jnp.einsum(
        "thgu,uhc->thgc",
        tree_weights.astype(jnp.bfloat16),
        new_values,
        preferred_element_type=jnp.float32,
    )
    denominator = denominator + jnp.sum(tree_weights, axis=-1)
    attended = (
        (numerator / denominator[..., None])
        .astype(jnp.bfloat16)
        .reshape(tree_size, head_count * 2 * HEAD_SIZE)
    )
    out_matrix = output_projection.reshape(head_count * 2 * HEAD_SIZE, output_projection.shape[2])
    attention_out = lax.psum_scatter(
        jnp.dot(attended, out_matrix, preferred_element_type=jnp.float32),
        "kv",
        scatter_dimension=0,
        tiled=True,
    )
    first_sum = (
        own_state.astype(jnp.float32)
        + attention_out * row_inverse(attention_out) * norm_post_attention
    ).astype(jnp.bfloat16)
    all_state = lax.all_gather(first_sum, ("kv", "vocab"), axis=0, tiled=True)
    all_float = all_state.astype(jnp.float32)
    scaled_ffn = (all_float * norm_pre_feedforward).astype(jnp.bfloat16)
    gate_up = jnp.einsum(
        "td,dcf->tcf", scaled_ffn, gate_up_weight, preferred_element_type=jnp.float32
    )
    ffn_squares = jnp.sum(all_float * all_float, axis=-1)
    gate_up, ffn_squares = lax.psum((gate_up, ffn_squares), "seq")
    activated = gated_units(gate_up, ffn_squares)
    ffn_out = lax.psum_scatter(
        jnp.dot(activated, down_weight, preferred_element_type=jnp.float32),
        ("kv", "vocab"),
        scatter_dimension=0,
        tiled=True,
    )
    first_float = first_sum.astype(jnp.float32)
    second_sum = (first_float + ffn_out * row_inverse(ffn_out) * norm_post_feedforward).astype(
        jnp.bfloat16
    )
    second_float = second_sum.astype(jnp.float32)
    normed = (second_float * row_inverse(second_float) * norm_final).astype(jnp.bfloat16)
    gathered = lax.all_gather(normed, ("kv", "vocab"), axis=0, tiled=True)
    lifted = jnp.einsum("td,ndc->tnc", gathered, draft_weight, preferred_element_type=jnp.float32)
    lifted = lax.psum(lifted.astype(jnp.bfloat16), "seq").astype(jnp.float32)
    branch = jax.nn.silu(lifted + draft_bias).astype(jnp.bfloat16)
    row_count = gathered.shape[0]
    vocab_rows = vocab_weight.shape[0]
    draft_count = branch.shape[1]
    columns = vocab_weight
    base_logits = lax.dot_general(
        lax.all_gather(gathered, "seq", axis=1, tiled=True),
        columns,
        (((1,), (1,)), ((), ())),
        preferred_element_type=jnp.float32,
    )
    columns = vocab_weight
    draft_extra = jnp.einsum(
        "tnc,vc->tnv",
        lax.all_gather(branch, ("kv", "vocab"), axis=2, tiled=True),
        columns,
        preferred_element_type=jnp.float32,
    )
    raw_logits = jnp.concatenate(
        [base_logits[:, None, :], base_logits[:, None, :] + draft_extra], axis=1
    )
    logits = LOGIT_CAP * jnp.tanh(raw_logits / LOGIT_CAP)
    totals = jnp.sum(jnp.exp(logits), axis=-1)
    head_total = draft_count + 1
    candidates = candidate_tokens.reshape(head_total, kv_count, tok_block, tenants, CAND)
    candidates = jnp.transpose(candidates, (0, 1, 3, 2, 4)).reshape(head_total, row_count, CAND)
    candidates = jnp.transpose(candidates, (1, 0, 2))
    vocab_start = lax.axis_index(("kv", "seq", "vocab")) * vocab_rows
    local_tokens = candidates - vocab_start
    entry_index = jnp.arange(vocab_rows, dtype=jnp.int32)
    picked = jnp.stack(
        [
            jnp.sum(
                jnp.where(entry_index == local_tokens[:, :, column : column + 1], logits, 0.0),
                axis=-1,
            )
            for column in range(CAND)
        ],
        axis=-1,
    )
    totals, picked = lax.psum((totals, picked), ("kv", "seq", "vocab"))
    log_totals = jnp.transpose(jnp.log(totals)).reshape(head_total, kv_count, tenants, tok_block)
    log_normalizer = jnp.transpose(log_totals, (0, 1, 3, 2)).reshape(head_total, tree_size, tenants)
    picked = jnp.transpose(picked, (1, 0, 2)).reshape(
        head_total, kv_count, tenants, tok_block, CAND
    )
    candidate_logits = jnp.transpose(picked, (0, 1, 3, 2, 4)).reshape(
        head_total, tree_size, tenants, CAND
    )
    accept_count = accepted_path.shape[1]
    slot_rows = length + jnp.arange(accept_count, dtype=jnp.int32)
    tree_nodes = jnp.arange(tree_size, dtype=jnp.int32)
    matches = (cache_cells[:, None, None] == slot_rows[None, :, None]) & (
        accepted_path[0][None, :, None] == tree_nodes[None, None, :]
    )
    selector = jnp.sum(matches.astype(jnp.float32), axis=1)
    written = jnp.sum(selector, axis=-1) > 0.0
    selector = selector.astype(jnp.bfloat16)

    def write_path(old_block, fresh_rows):
        moved_rows = jnp.dot(
            selector, fresh_rows.reshape(tree_size, -1), preferred_element_type=jnp.float32
        ).astype(jnp.bfloat16)
        return jnp.where(
            written[:, None], moved_rows, old_block[0].reshape(block_size, -1)
        ).reshape(old_block.shape)

    keys_updated = write_path(cache_keys, new_keys)
    values_updated = write_path(cache_values, new_values)
    return (keys_updated, values_updated, log_normalizer, candidate_logits)


def solution(mesh):
    placed = (
        P("kv", "vocab", "seq"),
        P("seq", "kv", None),
        P("kv", None, "seq"),
        P("seq"),
        P("seq"),
        P("seq"),
        P("seq"),
        P("seq"),
        P("vocab", "seq", "kv", None),
        P("vocab", "seq", "kv", None),
        P("vocab"),
        P("vocab", None, None),
        P("vocab", None),
        P("seq", None, ("kv", "vocab")),
        P(("kv", "vocab"), "seq"),
        P(None, "seq", ("kv", "vocab")),
        P(None, ("kv", "vocab")),
        P(("kv", "seq", "vocab"), None),
        P(),
    )
    return jax.shard_map(
        local,
        mesh=mesh,
        in_specs=placed,
        out_specs=(P("vocab", "seq", "kv", None), P("vocab", "seq", "kv", None), P(), P()),
        check_vma=False,
    )
```

profile of v0, /device:TPU:1, one launch (start us, length us, event | category | flops | bytes accessed | tf_op | source)
XLA Modules:
  0.0 775.7 jit_solution(17245792410160348582)
XLA Ops:
  7.2 0.8 copy.52
  8.1 15.8 %all-gather = bf16[48,1,448]{2,1,0:T(2,128)(2,1)S(1)} all-gather(bf16[6,1,448]{2,1,0:T(2,128)(2,1)S(1)} %copy.52), channel_id=2, replica_groups=mesh['kv'=8,'seq'=8,'vocab'=4] {'kv'}, dimensions={0}, use_global_device_ids=true | all-gather | bytes 48384 | tf_op jit(solution)/shard_map/all_gather | solution.py:73
  24.0 2.2 convolution_bitcast_fusion
  26.3 15.0 %psum.85 = f32[48]{0:T(128)S(1)} all-reduce(f32[48]{0:T(128)S(1)} %fusion.56), channel_id=1, replica_groups=mesh['kv'=8,'seq'=8,'vocab'=4] {'seq'}, use_global_device_ids=true, to_apply=%region_4.5 | all-reduce | flops 48 | bytes 384 | tf_op jit(solution)/shard_map/psum | solution.py:79
  42.0 0.7 compare_bitcast_fusion
  42.7 0.8 reduce_sum.178
  43.9 50.6 %all-reduce.10.cloned.1.call-done = f32[48,1,1024]{2,0,1:T(8,128)} async-done(((f32[48,1,1024]{2,0,1:T(8,128)}), f32[48,1,1024]{2,0,1:T(8,128)}) %all-reduce.10.cloned.1.call-update) | async-done | bytes 196624 | tf_op jit(solution)/shard_map/psum | solution.py:79
  94.5 1.0 broadcast_multiply_fusion
  95.8 1.2 fusion.93
  97.1 12.7 %psum.87 = f32[48,1,2]{0,2,1:T(2,128)S(1)} all-reduce(f32[48,1,2]{0,2,1:T(2,128)S(1)} %bitcast.224), channel_id=1, replica_groups=mesh['kv'=8,'seq'=8,'vocab'=4] {'seq'}, use_global_device_ids=true, to_apply=%region_8.9 | all-reduce | flops 96 | bytes 768 | tf_op jit(solution)/shard_map/psum | solution.py:108
  109.8 2.0 convolution_bitcast_fusion.1
  112.0 73.8 %all-reduce.12.cloned.1.call-done = f32[48,1,2,256]{3,0,2,1:T(8,128)} async-done(((f32[48,1,2,256]{3,0,2,1:T(8,128)}), f32[48,1,2,256]{3,0,2,1:T(8,128)}) %all-reduce.12.cloned.1.call-update) | async-done | bytes 98320 | tf_op jit(solution)/shard_map/psum | solution.py:108
  185.8 1.1 fusion.24
  187.0 0.2 fusion.35
  187.3 18.1 %fusion = f32[8,448]{1,0:T(8,128)S(1)} fusion(f32[48,448]{1,0:T(8,128)S(1)} %fusion.35), kind=kCustom, calls=%all-reduce-scatter | all-reduce-scatter fusion | flops 28673 | bytes 101376
  205.3 3.4 collective-permute-start
  208.8 1.6 collective-permute-start.1
  210.4 0.6 dynamic-slice.6
  212.0 11.6 %psum.88 = f32[6]{0:T(128)S(1)} all-reduce(f32[6]{0:T(128)S(1)} %multiply_reduce_fusion.2), channel_id=1, replica_groups=mesh['kv'=8,'seq'=8,'vocab'=4] {'seq'}, use_global_device_ids=true, to_apply=%region_12.13 | all-reduce | flops 6 | bytes 48 | tf_op jit(solution)/shard_map/psum | solution.py:36
  223.7 45.5 %all-gather.1 = bf16[32,6,448]{2,1,0:T(8,128)(2,1)S(1)} all-gather(bf16[1,6,448]{2,1,0:T(8,128)(2,1)S(1)} %bitcast.223), channel_id=1, replica_groups=mesh['kv'=8,'seq'=8,'vocab'=4] {'kv','vocab'}, dimensions={0}, use_global_device_ids=true | all-gather | bytes 177408 | tf_op jit(solution)/shard_map/all_gather | solution.py:136
  269.4 1.3 fusion.33
  270.8 11.5 %psum.90 = f32[192]{0:T(256)S(1)} all-reduce(f32[192]{0:T(256)S(1)} %multiply_reduce_fusion), channel_id=1, replica_groups=mesh['kv'=8,'seq'=8,'vocab'=4] {'seq'}, use_global_device_ids=true, to_apply=%region_15.16 | all-reduce | flops 192 | bytes 1536 | tf_op jit(solution)/shard_map/psum | solution.py:143
  282.3 57.1 %all-reduce.14.cloned.1.call-done = f32[192,2,448]{2,0,1:T(8,128)} async-done(((f32[192,2,448]{2,0,1:T(8,128)}), f32[192,2,448]{2,0,1:T(8,128)}) %all-reduce.14.cloned.1.call-update) | async-done | bytes 688144 | tf_op jit(solution)/shard_map/psum | solution.py:143
  339.4 1.6 fusion.53
  341.1 68.1 %fusion.1 = f32[8,448]{1,0:T(8,128)S(1)} fusion(f32[192,448]{1,0:T(8,128)S(1)} %fusion.53), kind=kCustom, calls=%all-reduce-scatter.1 | all-reduce-scatter fusion | flops 114689 | bytes 359424
  409.1 1.9 collective-permute-start.2
  411.1 1.9 collective-permute-start.3
  413.0 1.4 collective-permute-start.9
  414.4 1.9 collective-permute-start.4
  416.4 1.9 collective-permute-start.5
  418.3 5.9 collective-permute-start.6
  424.2 6.8 collective-permute-start.7
  431.0 3.9 collective-permute-start.8
  435.0 0.6 dynamic-slice.10
  436.3 0.8 concatenate.35
  437.2 12.6 %psum.91 = f32[6]{0:T(128)S(1)} all-reduce(f32[6]{0:T(128)S(1)} %multiply_reduce_fusion.1), channel_id=1, replica_groups=mesh['kv'=8,'seq'=8,'vocab'=4] {'seq'}, use_global_device_ids=true, to_apply=%region_18.19 | all-reduce | flops 6 | bytes 48 | tf_op jit(solution)/shard_map/psum | solution.py:36
  450.0 10.7 %psum.92 = f32[6]{0:T(128)S(1)} all-reduce(f32[6]{0:T(128)S(1)} %get-tuple-element.17), channel_id=1, replica_groups=mesh['kv'=8,'seq'=8,'vocab'=4] {'seq'}, use_global_device_ids=true, to_apply=%region_20.21 | all-reduce | flops 6 | bytes 48 | tf_op jit(solution)/shard_map/psum | solution.py:36
  460.8 48.2 %all-gather.2 = bf16[32,6,448]{2,1,0:T(8,128)(2,1)S(1)} all-gather(bf16[1,6,448]{2,1,0:T(8,128)(2,1)S(1)} %fusion.82), channel_id=1, replica_groups=mesh['kv'=8,'seq'=8,'vocab'=4] {'kv','vocab'}, dimensions={0}, use_global_device_ids=true | all-gather | bytes 177408 | tf_op jit(solution)/shard_map/all_gather | solution.py:157
  509.1 0.9 convolution_convert_fusion.2
  510.2 0.8 reshape.410
  511.0 0.2 all-gather.7.cloned.1.call-start
  511.2 64.1 %all-reduce.16.cloned.1.call-done = bf16[192,4,112]{2,0,1:T(8,128)(2,1)} async-done(((bf16[192,4,112]{2,0,1:T(8,128)(2,1)}), bf16[192,4,112]{2,0,1:T(8,128)(2,1)}) %all-reduce.16.cloned.1.call-update) | async-done | bytes 172048 | tf_op jit(solution)/shard_map/psum | solution.py:159
  575.3 1.0 multiply_convert_fusion
  576.3 0.9 copy.60
  577.5 0.4 copy.63
  577.9 0.6 sub.35
  578.7 0.3 convert_reduce_fusion
  579.1 0.6 copy_bitcast_fusion
  579.7 0.6 copy_bitcast_fusion.2
  580.3 0.6 copy_bitcast_fusion.4
  580.9 0.6 copy_bitcast_fusion.6
  581.5 2.5 fusion.6
  584.1 1.5 fusion.8
  585.5 30.5 %all-gather.9.cloned.1.call-done = bf16[8,448,192]{1,2,0:T(8,128)(2,1)} async-done(((bf16[1,448,192]{1,2,0:T(8,128)(2,1)}), bf16[8,448,192]{1,2,0:T(8,128)(2,1)}) %all-gather.9.cloned.1.call-update) | async-done | bytes 1376272 | tf_op jit(solution)/shard_map/all_gather | solution.py:166
  616.1 2.3 copy.59
  618.4 2.7 reshape.412
  621.1 3.8 fusion.95
  625.0 52.4 %all-gather.7.cloned.1.call-done = bf16[192,4,3584]{0,1,2:T(4,128)(2,1)} async-done(((bf16[192,4,112]{0,1,2:T(4,128)(2,1)}), bf16[192,4,3584]{0,1,2:T(4,128)(2,1)}) %all-gather.7.cloned.1.call-update) | async-done | bytes 5505040 | tf_op jit(solution)/shard_map/all_gather | solution.py:174
  677.3 8.2 %fusion.17 = f32[192,4,512]{2,0,1:T(8,128)S(1)} fusion(bf16[512,3584]{1,0:T(8,128)(2,1)} %param.36, bf16[192,4,3584]{0,1,2:T(4,128)(2,1)} %all-gather.7.cloned.1.call-done, f32[192,512]{1,0:T(8,128)S(1)} %fusion.95), kind=kOutput, calls=%fused_computation.38 | convolution fusion | flops 2818965504 | bytes 11141120 | tf_op jit(solution)/shard_map/tnc,vc->tnv/dot_general | solution.py:172
  685.6 4.4 select_reduce_fusion
  690.2 0.8 reshape.400
  691.2 0.2 reshape.401
  691.4 76.6 %all-reduce.4 = (f32[192,5]{0,1:T(8,128)S(1)}, f32[5,48,4,8]{1,3,2,0:T(8,128)}) all-reduce(f32[192,5]{0,1:T(8,128)S(1)} %get-tuple-element.19, f32[5,48,4,8]{1,3,2,0:T(8,128)S(1)} %reshape.401), channel_id=1, replica_groups=mesh['kv'=8,'seq'=8,'vocab'=4] {'kv','seq','vocab'}, use_global_device_ids=true, to_apply=%region_23.24 | all-reduce | flops 8640 | bytes 69120 | tf_op jit(solution)/shard_map/psum | solution.py:200
  768.1 0.7 reshape.399
  (118 shorter events, 3.5 us)
Async XLA Ops:
  7.2 262.2 %copy-start = (bf16[448,2,448]{2,1,0:T(2,128)(2,1)S(1)}, bf16[448,2,448]{2,1,0:T(2,128)(2,1)}, u32[]{:S(2)}) copy-start(bf16[448,2,448]{2,1,0:T(2,128)(2,1)} %param.32) | copy-start | bytes 2408452
  7.2 88.7 %copy-start.2 = (bf16[1,2048,1,256]{3,1,2,0:T(8,128)(2,1)S(1)}, bf16[1,2048,1,256]{3,1,2,0:T(8,128)(2,1)}, u32[]{:S(2)}) copy-start(bf16[1,2048,1,256]{3,1,2,0:T(8,128)(2,1)} %param.27) | copy-start | bytes 3145732
  7.2 87.3 %all-reduce.10.cloned.1.call-start = ((), (), s32[]{:S(2)}) async-start(), calls=%async_computation | async-start | bytes 393216 | tf_op jit(solution)/shard_map/psum | solution.py:79
  26.1 83.6 %copy-start.1 = (bf16[1,2048,1,256]{3,1,2,0:T(8,128)(2,1)S(1)}, bf16[1,2048,1,256]{3,1,2,0:T(8,128)(2,1)}, u32[]{:S(2)}) copy-start(bf16[1,2048,1,256]{3,1,2,0:T(8,128)(2,1)} %param.28) | copy-start | bytes 3145732
  26.2 159.7 %all-reduce.12.cloned.1.call-start = ((), (), s32[]{:S(2)}) async-start(), calls=%async_computation.1 | async-start | bytes 196608 | tf_op jit(solution)/shard_map/psum | solution.py:108
  97.1 89.9 %copy-start.3 = (bf16[1,512,448]{1,2,0:T(8,128)(2,1)S(1)}, bf16[1,512,448]{1,2,0:T(8,128)(2,1)}, u32[]{:S(2)}) copy-start(bf16[1,512,448]{1,2,0:T(8,128)(2,1)} %param.21) | copy-start | bytes 1376260
  97.1 113.3 %copy-start.20 = (u32[256]{0:T(256)S(1)}, u32[256]{0:T(256)}, u32[]{:S(2)}) copy-start(u32[256]{0:T(256)} %constant.87) | copy-start | bytes 3076
  97.1 126.5 %copy-start.13 = (bf16[6,1,448]{2,0,1:T(8,128)(2,1)S(1)}, bf16[6,1,448]{2,0,1:T(8,128)(2,1)}, u32[]{:S(2)}) copy-start(bf16[6,1,448]{2,0,1:T(8,128)(2,1)} %param.19) | copy-start | bytes 16132
  97.1 126.5 %copy-start.16 = (f32[448]{0:T(512)S(1)}, f32[448]{0:T(512)}, u32[]{:S(2)}) copy-start(f32[448]{0:T(512)} %param.23) | copy-start | bytes 5380
  109.8 159.6 %copy-start.14 = (f32[448]{0:T(512)S(1)}, f32[448]{0:T(512)}, u32[]{:S(2)}) copy-start(f32[448]{0:T(512)} %param.24) | copy-start | bytes 5380
  111.8 227.7 %all-reduce.14.cloned.1.call-start = ((), (), s32[]{:S(2)}) async-start(), calls=%async_computation.2 | async-start | bytes 1572864 | tf_op jit(solution)/shard_map/psum | solution.py:143
  205.3 6.3 collective-permute-start
  208.8 2.8 collective-permute-start.1
  270.6 164.4 %copy-start.19 = (u32[256]{0:T(256)S(1)}, u32[256]{0:T(256)}, u32[]{:S(2)}) copy-start(u32[256]{0:T(256)} %constant.91) | copy-start | bytes 3076
  270.6 179.2 %copy-start.17 = (f32[448]{0:T(512)S(1)}, f32[448]{0:T(512)}, u32[]{:S(2)}) copy-start(f32[448]{0:T(512)} %param.25) | copy-start | bytes 5380
  270.6 190.1 %copy-start.18 = (f32[448]{0:T(512)S(1)}, f32[448]{0:T(512)}, u32[]{:S(2)}) copy-start(f32[448]{0:T(512)} %param.26) | copy-start | bytes 5380
  270.6 238.5 %copy-start.4 = (bf16[4,448,112]{2,1,0:T(8,128)(2,1)S(1)}, bf16[4,448,112]{2,1,0:T(8,128)(2,1)}, u32[]{:S(2)}) copy-start(bf16[4,448,112]{2,1,0:T(8,128)(2,1)} %param.34) | copy-start | bytes 1204228
  270.7 304.6 %all-reduce.16.cloned.1.call-start = ((), (), s32[]{:S(2)}) async-start(), calls=%async_computation.3 | async-start | bytes 393216 | tf_op jit(solution)/shard_map/psum | solution.py:159
  341.1 234.2 %copy-start.15 = (f32[4,112]{1,0:T(4,128)S(1)}, f32[4,112]{1,0:T(4,128)}, u32[]{:S(2)}) copy-start(f32[4,112]{1,0:T(4,128)} %param.35) | copy-start | bytes 5380
  409.1 15.1 %collective-permute-start.2 = (f32[8,448]{1,0:T(8,128)S(1)}, f32[8,448]{1,0:T(8,128)S(1)}, u32[]{:S(2)}, u32[]{:S(2)}) collective-permute-start(f32[8,448]{1,0:T(8,128)S(1)} %fusion.1), channel_id=1, source_target_pairs={{0,1},{1,2},{2,3},{3,32},{32,33},{33,34},{34,35},{35,64},{64,65},{... | collective-permute-start | bytes 43016
  411.1 20.0 %collective-permute-start.3 = (f32[8,448]{1,0:T(8,128)S(1)}, f32[8,448]{1,0:T(8,128)S(1)}, u32[]{:S(2)}, u32[]{:S(2)}) collective-permute-start(f32[8,448]{1,0:T(8,128)S(1)} %fusion.1), channel_id=1, source_target_pairs={{0,2},{1,3},{2,32},{3,33},{32,34},{33,35},{34,64},{35,65},{64,66},... | collective-permute-start | bytes 43016
  413.0 164.3 %copy-start.5 = (s32[5,48,4,8]{1,3,2,0:T(8,128)S(1)}, s32[5,48,4,8]{1,3,2,0:T(8,128)}, u32[]{:S(2)}) copy-start(s32[5,48,4,8]{1,3,2,0:T(8,128)} %param.37) | copy-start | bytes 92164
  413.0 5.3 collective-permute-start.9
  414.4 21.8 %collective-permute-start.4 = (f32[8,448]{1,0:T(8,128)S(1)}, f32[8,448]{1,0:T(8,128)S(1)}, u32[]{:S(2)}, u32[]{:S(2)}) collective-permute-start(f32[8,448]{1,0:T(8,128)S(1)} %fusion.1), channel_id=1, source_target_pairs={{0,3},{1,32},{2,33},{3,34},{32,35},{33,64},{34,65},{35,66},{64,67}... | collective-permute-start | bytes 43016
  416.4 19.9 %collective-permute-start.5 = (f32[8,448]{1,0:T(8,128)S(1)}, f32[8,448]{1,0:T(8,128)S(1)}, u32[]{:S(2)}, u32[]{:S(2)}) collective-permute-start(f32[8,448]{1,0:T(8,128)S(1)} %fusion.1), channel_id=1, source_target_pairs={{0,32},{1,33},{2,34},{3,35},{32,64},{33,65},{34,66},{35,67},{64,96... | collective-permute-start | bytes 43016
  418.3 17.9 %collective-permute-start.6 = (f32[8,448]{1,0:T(8,128)S(1)}, f32[8,448]{1,0:T(8,128)S(1)}, u32[]{:S(2)}, u32[]{:S(2)}) collective-permute-start(f32[8,448]{1,0:T(8,128)S(1)} %fusion.1), channel_id=1, source_target_pairs={{0,33},{1,34},{2,35},{3,64},{32,65},{33,66},{34,67},{35,96},{64,97... | collective-permute-start | bytes 43016
  424.2 12.1 %collective-permute-start.7 = (f32[8,448]{1,0:T(8,128)S(1)}, f32[8,448]{1,0:T(8,128)S(1)}, u32[]{:S(2)}, u32[]{:S(2)}) collective-permute-start(f32[8,448]{1,0:T(8,128)S(1)} %fusion.1), channel_id=1, source_target_pairs={{0,34},{1,35},{2,64},{3,65},{32,66},{33,67},{34,96},{35,97},{64,98... | collective-permute-start | bytes 43016
  431.0 5.2 collective-permute-start.8
  510.1 106.0 %all-gather.9.cloned.1.call-start = ((), (), s32[]{:S(2)}) async-start(), calls=%async_computation.5 | async-start | bytes 1769472 | tf_op jit(solution)/shard_map/all_gather | solution.py:166
  511.0 67.6 %copy-start.21 = (s32[1,5]{1,0:T(1,128)S(1)}, s32[1,5]{1,0:T(1,128)}, u32[]{:S(2)}) copy-start(s32[1,5]{1,0:T(1,128)} %param.31) | copy-start | bytes 64
  511.0 166.3 %all-gather.7.cloned.1.call-start = ((), (), s32[]{:S(2)}) async-start(), calls=%async_computation.4 | async-start | bytes 7569408 | tf_op jit(solution)/shard_map/all_gather | solution.py:174
  624.9 60.7 %copy-start.6 = (s32[192,5]{0,1:T(8,128)S(1)}, s32[192,5]{0,1:T(8,128)}, u32[]{:S(2)}) copy-start(s32[192,5]{0,1:T(8,128)} %get-tuple-element.43) | copy-start | bytes 11524
  624.9 60.7 %copy-start.7 = (s32[192,5]{0,1:T(8,128)S(1)}, s32[192,5]{0,1:T(8,128)}, u32[]{:S(2)}) copy-start(s32[192,5]{0,1:T(8,128)} %get-tuple-element.44) | copy-start | bytes 11524
  624.9 60.7 %copy-start.8 = (s32[192,5]{0,1:T(8,128)S(1)}, s32[192,5]{0,1:T(8,128)}, u32[]{:S(2)}) copy-start(s32[192,5]{0,1:T(8,128)} %get-tuple-element.45) | copy-start | bytes 11524
  624.9 60.7 %copy-start.9 = (s32[192,5]{0,1:T(8,128)S(1)}, s32[192,5]{0,1:T(8,128)}, u32[]{:S(2)}) copy-start(s32[192,5]{0,1:T(8,128)} %get-tuple-element.46) | copy-start | bytes 11524
  624.9 60.7 %copy-start.10 = (s32[192,5]{0,1:T(8,128)S(1)}, s32[192,5]{0,1:T(8,128)}, u32[]{:S(2)}) copy-start(s32[192,5]{0,1:T(8,128)} %get-tuple-element.47) | copy-start | bytes 11524
  624.9 60.7 %copy-start.11 = (s32[192,5]{0,1:T(8,128)S(1)}, s32[192,5]{0,1:T(8,128)}, u32[]{:S(2)}) copy-start(s32[192,5]{0,1:T(8,128)} %get-tuple-element.48) | copy-start | bytes 11524
  625.0 60.7 %copy-start.12 = (s32[192,5]{0,1:T(8,128)S(1)}, s32[192,5]{0,1:T(8,128)}, u32[]{:S(2)}) copy-start(s32[192,5]{0,1:T(8,128)} %get-tuple-element.49) | copy-start | bytes 11524
Sparse Core Ops, SparseCore 0:
  26.3 68.1 all-reduce.9
  111.9 73.9 all-reduce.11
  270.8 68.6 all-reduce.13
  510.2 65.0 all-reduce.15
  576.9 39.1 all-gather.8
  618.5 58.7 all-gather.6
where the time goes:
time: 777 us; the launch traced here: 776 us
  blocking collectives  346 us (45%)
  waiting for transfers between devices  329 us (42%)
  starting transfers between devices  31.2 us (4%)
  matrix products  26.7 us (3%)
  between operations  16.9 us (2%)
  local copies, waits for them, and re-layouts  16 us (2%)
  other arithmetic  9.93 us (1%)
    unnamed x2, blocking collectives  86.2 us
    psum x1, blocking collectives, local(): totals, picked = lax.psum((totals, picked), ('kv', 'seq', 'vocab'))  76.6 us
    psum x1, waiting for transfers between devices, local(): lax.psum((numerator, jnp.sum(weights, axis=-1)), 'seq')  73.8 us
    psum x1, waiting for transfers between devices, local(): lifted = lax.psum(lifted.astype(jnp.bfloat16), 'seq').astype(jnp.float32)  64.1 us
    psum x1, waiting for transfers between devices, local(): gate_up, ffn_squares = lax.psum((gate_up, ffn_squares), 'seq')  57.1 us
    all_gather x1, waiting for transfers between devices, local(): lax.all_gather(branch, ('kv', 'vocab'), axis=2, tiled=True)  52.4 us
    psum x1, waiting for transfers between devices, local(): lax.psum((projected_rows, jnp.sum(tenant_float * tenant_float, axis=-1)),...  50.6 us
    all_gather x1, blocking collectives, local(): gathered = lax.all_gather(normed, ('kv', 'vocab'), axis=0, tiled=True)  48.2 us
  transfers between devices with their start and end apart: 16, of which 6 were waited for; matrix products, arithmetic and copies ran while one was open for 3% of the time, Pallas kernels for 0%

commit v1 on v0

--- a/solution.py
+++ b/solution.py
@@ -33,7 +33,9 @@
 
 
 def row_inverse(values):
-    totals = lax.psum(jnp.sum(values * values, axis=-1), "seq")
+    x = jnp.sum(values * values, axis=-1)
+    parts = lax.all_gather(x, "seq", axis=0, tiled=False)
+    totals = parts.sum(axis=0)
     return lax.rsqrt(totals / MODEL_WIDTH + EPSILON)[:, None]
 
 

time: 777 us -> 779 us (level)
    psum x3 -> x0, blocking collectives: 34.9 us -> none  [row_inverse(): totals = lax.psum(jnp.sum(values * values, axis=-1), 'seq')]
    unnamed x2 -> x5, blocking collectives: 86.2 us -> 121 us
where the time goes in v1:
time: 779 us; the launch traced here: 778 us
  blocking collectives  346 us (44%)
  waiting for transfers between devices  329 us (42%)
  starting transfers between devices  31 us (4%)
  matrix products  26.7 us (3%)
  local copies, waits for them, and re-layouts  17.6 us (2%)
  between operations  17.6 us (2%)
  other arithmetic  10 us (1%)
    unnamed x5, blocking collectives  121 us
    psum x1, blocking collectives, local(): totals, picked = lax.psum((totals, picked), ('kv', 'seq', 'vocab'))  76.6 us
    psum x1, waiting for transfers between devices, local(): lax.psum((numerator, jnp.sum(weights, axis=-1)), 'seq')  73.9 us
    psum x1, waiting for transfers between devices, local(): lifted = lax.psum(lifted.astype(jnp.bfloat16), 'seq').astype(jnp.float32)  64.1 us
    psum x1, waiting for transfers between devices, local(): gate_up, ffn_squares = lax.psum((gate_up, ffn_squares), 'seq')  57 us
    all_gather x1, waiting for transfers between devices, local(): lax.all_gather(branch, ('kv', 'vocab'), axis=2, tiled=True)  52.4 us
    psum x1, waiting for transfers between devices, local(): lax.psum((projected_rows, jnp.sum(tenant_float * tenant_float, axis=-1)),...  50.6 us
    all_gather x1, blocking collectives, local(): gathered = lax.all_gather(normed, ('kv', 'vocab'), axis=0, tiled=True)  48.2 us
  transfers between devices with their start and end apart: 16, of which 6 were waited for; matrix products, arithmetic and copies ran while one was open for 3% of the time, Pallas kernels for 0%

profile of v1, /device:TPU:1, one launch (start us, length us, event | category | flops | bytes accessed | tf_op | source)
XLA Modules:
  0.0 777.7 jit_solution(16809206044186764168)
XLA Ops:
  7.2 0.8 copy.52
  8.1 15.8 %all-gather = bf16[48,1,448]{2,1,0:T(2,128)(2,1)S(1)} all-gather(bf16[6,1,448]{2,1,0:T(2,128)(2,1)S(1)} %copy.52), channel_id=2, replica_groups=mesh['kv'=8,'seq'=8,'vocab'=4] {'kv'}, dimensions={0}, use_global_device_ids=true | all-gather | bytes 48384 | tf_op jit(solution)/shard_map/all_gather | solution.py:75
  24.0 2.2 convolution_bitcast_fusion
  26.3 15.0 %psum.64 = f32[48]{0:T(128)S(1)} all-reduce(f32[48]{0:T(128)S(1)} %fusion.56), channel_id=1, replica_groups=mesh['kv'=8,'seq'=8,'vocab'=4] {'seq'}, use_global_device_ids=true, to_apply=%region_4.5 | all-reduce | flops 48 | bytes 384 | tf_op jit(solution)/shard_map/psum | solution.py:81
  42.0 0.7 compare_bitcast_fusion
  42.7 0.8 reduce_sum.205
  43.9 50.6 %all-reduce.13.cloned.1.call-done = f32[48,1,1024]{2,0,1:T(8,128)} async-done(((f32[48,1,1024]{2,0,1:T(8,128)}), f32[48,1,1024]{2,0,1:T(8,128)}) %all-reduce.13.cloned.1.call-update) | async-done | bytes 196624 | tf_op jit(solution)/shard_map/psum | solution.py:81
  94.5 1.0 broadcast_multiply_fusion
  95.8 1.2 fusion.93
  97.1 12.7 %psum.66 = f32[48,1,2]{0,2,1:T(2,128)S(1)} all-reduce(f32[48,1,2]{0,2,1:T(2,128)S(1)} %bitcast.225), channel_id=1, replica_groups=mesh['kv'=8,'seq'=8,'vocab'=4] {'seq'}, use_global_device_ids=true, to_apply=%region_8.9 | all-reduce | flops 96 | bytes 768 | tf_op jit(solution)/shard_map/psum | solution.py:110
  109.8 2.0 convolution_bitcast_fusion.1
  112.0 73.9 %all-reduce.15.cloned.1.call-done = f32[48,1,2,256]{3,0,2,1:T(8,128)} async-done(((f32[48,1,2,256]{3,0,2,1:T(8,128)}), f32[48,1,2,256]{3,0,2,1:T(8,128)}) %all-reduce.15.cloned.1.call-update) | async-done | bytes 98320 | tf_op jit(solution)/shard_map/psum | solution.py:110
  185.9 1.1 fusion.24
  187.3 18.1 %fusion = f32[8,448]{1,0:T(8,128)S(1)} fusion(f32[48,448]{1,0:T(8,128)S(1)} %fusion.35), kind=kCustom, calls=%all-reduce-scatter | all-reduce-scatter fusion | flops 28673 | bytes 101376
  205.4 3.4 collective-permute-start
  208.9 1.6 collective-permute-start.1
  210.4 0.6 dynamic-slice.9
  211.7 0.6 dynamic-slice
  213.3 0.2 dynamic-update-slice
  213.5 11.5 %all-reduce = f32[48]{0:T(128)S(1)} all-reduce(f32[48]{0:T(128)S(1)} %dynamic-update-slice), channel_id=3, replica_groups=mesh['kv'=8,'seq'=8,'vocab'=4] {'seq'}, use_global_device_ids=true, to_apply=%add | all-reduce | flops 48 | bytes 384
  225.2 45.5 %all-gather.4 = bf16[32,6,448]{2,1,0:T(8,128)(2,1)S(1)} all-gather(bf16[1,6,448]{2,1,0:T(8,128)(2,1)S(1)} %bitcast.224), channel_id=1, replica_groups=mesh['kv'=8,'seq'=8,'vocab'=4] {'kv','vocab'}, dimensions={0}, use_global_device_ids=true | all-gather | bytes 177408 | tf_op jit(solution)/shard_map/all_gather | solution.py:138
  270.9 1.3 fusion.33
  272.3 11.5 %psum.68 = f32[192]{0:T(256)S(1)} all-reduce(f32[192]{0:T(256)S(1)} %multiply_reduce_fusion), channel_id=1, replica_groups=mesh['kv'=8,'seq'=8,'vocab'=4] {'seq'}, use_global_device_ids=true, to_apply=%region_15.16 | all-reduce | flops 192 | bytes 1536 | tf_op jit(solution)/shard_map/psum | solution.py:145
  283.8 57.0 %all-reduce.17.cloned.1.call-done = f32[192,2,448]{2,0,1:T(8,128)} async-done(((f32[192,2,448]{2,0,1:T(8,128)}), f32[192,2,448]{2,0,1:T(8,128)}) %all-reduce.17.cloned.1.call-update) | async-done | bytes 688144 | tf_op jit(solution)/shard_map/psum | solution.py:145
  340.9 1.6 fusion.53
  342.5 68.1 %fusion.1 = f32[8,448]{1,0:T(8,128)S(1)} fusion(f32[192,448]{1,0:T(8,128)S(1)} %fusion.53), kind=kCustom, calls=%all-reduce-scatter.1 | all-reduce-scatter fusion | flops 114689 | bytes 359424
  410.6 1.9 collective-permute-start.2
  412.5 1.9 collective-permute-start.3
  414.5 1.3 collective-permute-start.9
  415.8 1.9 collective-permute-start.4
  417.7 1.9 collective-permute-start.5
  419.6 5.9 collective-permute-start.6
  425.5 6.8 collective-permute-start.7
  432.4 3.9 collective-permute-start.8
  436.3 0.6 dynamic-slice.13
  437.6 0.8 concatenate.35
  438.5 0.2 dynamic-update-slice.1
  438.8 12.6 %all-reduce.1 = f32[48]{0:T(128)S(1)} all-reduce(f32[48]{0:T(128)S(1)} %dynamic-update-slice.1), channel_id=4, replica_groups=mesh['kv'=8,'seq'=8,'vocab'=4] {'seq'}, use_global_device_ids=true, to_apply=%add.1 | all-reduce | flops 48 | bytes 384
  451.9 10.7 %all-reduce.2 = f32[48]{0:T(128)S(1)} all-reduce(f32[48]{0:T(128)S(1)} %dynamic-update-slice.2), channel_id=5, replica_groups=mesh['kv'=8,'seq'=8,'vocab'=4] {'seq'}, use_global_device_ids=true, to_apply=%add.2 | all-reduce | flops 48 | bytes 384
  462.8 48.2 %all-gather.5 = bf16[32,6,448]{2,1,0:T(8,128)(2,1)S(1)} all-gather(bf16[1,6,448]{2,1,0:T(8,128)(2,1)S(1)} %fusion.82), channel_id=1, replica_groups=mesh['kv'=8,'seq'=8,'vocab'=4] {'kv','vocab'}, dimensions={0}, use_global_device_ids=true | all-gather | bytes 177408 | tf_op jit(solution)/shard_map/all_gather | solution.py:159
  511.1 0.9 convolution_convert_fusion.2
  512.2 0.8 reshape.434
  513.2 64.1 %all-reduce.19.cloned.1.call-done = bf16[192,4,112]{2,0,1:T(8,128)(2,1)} async-done(((bf16[192,4,112]{2,0,1:T(8,128)(2,1)}), bf16[192,4,112]{2,0,1:T(8,128)(2,1)}) %all-reduce.19.cloned.1.call-update) | async-done | bytes 172048 | tf_op jit(solution)/shard_map/psum | solution.py:161
  577.3 1.0 multiply_convert_fusion
  578.3 0.9 copy.60
  579.5 0.4 copy.63
  579.9 0.6 sub.35
  580.7 0.3 convert_reduce_fusion
  581.1 0.6 copy_bitcast_fusion
  581.7 0.6 copy_bitcast_fusion.2
  582.3 0.6 copy_bitcast_fusion.4
  582.9 0.6 copy_bitcast_fusion.6
  583.5 2.5 fusion.6
  586.0 1.5 fusion.8
  587.5 30.6 %all-gather.12.cloned.1.call-done = bf16[8,448,192]{1,2,0:T(8,128)(2,1)} async-done(((bf16[1,448,192]{1,2,0:T(8,128)(2,1)}), bf16[8,448,192]{1,2,0:T(8,128)(2,1)}) %all-gather.12.cloned.1.call-update) | async-done | bytes 1376272 | tf_op jit(solution)/shard_map/all_gather | solution.py:168
  618.1 2.3 copy.59
  620.4 2.7 reshape.436
  623.1 3.8 fusion.95
  627.0 52.4 %all-gather.10.cloned.1.call-done = bf16[192,4,3584]{0,1,2:T(4,128)(2,1)} async-done(((bf16[192,4,112]{0,1,2:T(4,128)(2,1)}), bf16[192,4,3584]{0,1,2:T(4,128)(2,1)}) %all-gather.10.cloned.1.call-update) | async-done | bytes 5505040 | tf_op jit(solution)/shard_map/all_gather | solution.py:176
  679.3 8.2 %fusion.17 = f32[192,4,512]{2,0,1:T(8,128)S(1)} fusion(bf16[512,3584]{1,0:T(8,128)(2,1)} %param.36, bf16[192,4,3584]{0,1,2:T(4,128)(2,1)} %all-gather.10.cloned.1.call-done, f32[192,512]{1,0:T(8,128)S(1)} %fusion.95), kind=kOutput, calls=%fused_computation.38 | convolution fusion | flops 2818965504 | bytes 11141120 | tf_op jit(solution)/shard_map/tnc,vc->tnv/dot_general | solution.py:174
  687.6 4.4 select_reduce_fusion
  692.2 0.8 reshape.412
  693.4 76.6 %all-reduce.7 = (f32[192,5]{0,1:T(8,128)S(1)}, f32[5,48,4,8]{1,3,2,0:T(8,128)}) all-reduce(f32[192,5]{0,1:T(8,128)S(1)} %get-tuple-element.19, f32[5,48,4,8]{1,3,2,0:T(8,128)S(1)} %reshape.413), channel_id=1, replica_groups=mesh['kv'=8,'seq'=8,'vocab'=4] {'kv','seq','vocab'}, use_global_device_ids=true, to_apply=%region_23.24 | all-reduce | flops 8640 | bytes 69120 | tf_op jit(solution)/shard_map/psum | solution.py:202
  770.1 0.7 reshape.411
  (133 shorter events, 4.7 us)
Async XLA Ops:
  7.2 263.7 %copy-start = (bf16[448,2,448]{2,1,0:T(2,128)(2,1)S(1)}, bf16[448,2,448]{2,1,0:T(2,128)(2,1)}, u32[]{:S(2)}) copy-start(bf16[448,2,448]{2,1,0:T(2,128)(2,1)} %param.32) | copy-start | bytes 2408452
  7.2 88.7 %copy-start.2 = (bf16[1,2048,1,256]{3,1,2,0:T(8,128)(2,1)S(1)}, bf16[1,2048,1,256]{3,1,2,0:T(8,128)(2,1)}, u32[]{:S(2)}) copy-start(bf16[1,2048,1,256]{3,1,2,0:T(8,128)(2,1)} %param.27) | copy-start | bytes 3145732
  7.2 87.3 %all-reduce.13.cloned.1.call-start = ((), (), s32[]{:S(2)}) async-start(), calls=%async_computation | async-start | bytes 393216 | tf_op jit(solution)/shard_map/psum | solution.py:81
  26.1 83.6 %copy-start.1 = (bf16[1,2048,1,256]{3,1,2,0:T(8,128)(2,1)S(1)}, bf16[1,2048,1,256]{3,1,2,0:T(8,128)(2,1)}, u32[]{:S(2)}) copy-start(bf16[1,2048,1,256]{3,1,2,0:T(8,128)(2,1)} %param.28) | copy-start | bytes 3145732
  26.2 159.7 %all-reduce.15.cloned.1.call-start = ((), (), s32[]{:S(2)}) async-start(), calls=%async_computation.1 | async-start | bytes 196608 | tf_op jit(solution)/shard_map/psum | solution.py:110
  97.1 90.0 %copy-start.3 = (bf16[1,512,448]{1,2,0:T(8,128)(2,1)S(1)}, bf16[1,512,448]{1,2,0:T(8,128)(2,1)}, u32[]{:S(2)}) copy-start(bf16[1,512,448]{1,2,0:T(8,128)(2,1)} %param.21) | copy-start | bytes 1376260
  97.1 113.3 %copy-start.20 = (u32[256]{0:T(256)S(1)}, u32[256]{0:T(256)}, u32[]{:S(2)}) copy-start(u32[256]{0:T(256)} %constant.105) | copy-start | bytes 3076
  97.1 114.6 %copy-start.22 = (u32[256]{0:T(256)S(1)}, u32[256]{0:T(256)}, u32[]{:S(2)}) copy-start(u32[256]{0:T(256)} %constant.87) | copy-start | bytes 3076
  97.1 128.0 %copy-start.13 = (bf16[6,1,448]{2,0,1:T(8,128)(2,1)S(1)}, bf16[6,1,448]{2,0,1:T(8,128)(2,1)}, u32[]{:S(2)}) copy-start(bf16[6,1,448]{2,0,1:T(8,128)(2,1)} %param.19) | copy-start | bytes 16132
  97.1 128.0 %copy-start.16 = (f32[448]{0:T(512)S(1)}, f32[448]{0:T(512)}, u32[]{:S(2)}) copy-start(f32[448]{0:T(512)} %param.23) | copy-start | bytes 5380
  109.8 161.1 %copy-start.14 = (f32[448]{0:T(512)S(1)}, f32[448]{0:T(512)}, u32[]{:S(2)}) copy-start(f32[448]{0:T(512)} %param.24) | copy-start | bytes 5380
  111.8 229.1 %all-reduce.17.cloned.1.call-start = ((), (), s32[]{:S(2)}) async-start(), calls=%async_computation.2 | async-start | bytes 1572864 | tf_op jit(solution)/shard_map/psum | solution.py:145
  205.4 7.6 collective-permute-start
  208.9 4.1 collective-permute-start.1
  272.1 164.2 %copy-start.19 = (u32[256]{0:T(256)S(1)}, u32[256]{0:T(256)}, u32[]{:S(2)}) copy-start(u32[256]{0:T(256)} %constant.109) | copy-start | bytes 3076
  272.1 179.4 %copy-start.17 = (f32[448]{0:T(512)S(1)}, f32[448]{0:T(512)}, u32[]{:S(2)}) copy-start(f32[448]{0:T(512)} %param.25) | copy-start | bytes 5380
  272.1 190.6 %copy-start.18 = (f32[448]{0:T(512)S(1)}, f32[448]{0:T(512)}, u32[]{:S(2)}) copy-start(f32[448]{0:T(512)} %param.26) | copy-start | bytes 5380
  272.1 239.0 %copy-start.4 = (bf16[4,448,112]{2,1,0:T(8,128)(2,1)S(1)}, bf16[4,448,112]{2,1,0:T(8,128)(2,1)}, u32[]{:S(2)}) copy-start(bf16[4,448,112]{2,1,0:T(8,128)(2,1)} %param.34) | copy-start | bytes 1204228
  272.2 305.1 %all-reduce.19.cloned.1.call-start = ((), (), s32[]{:S(2)}) async-start(), calls=%async_computation.3 | async-start | bytes 393216 | tf_op jit(solution)/shard_map/psum | solution.py:161
  342.5 234.8 %copy-start.15 = (f32[4,112]{1,0:T(4,128)S(1)}, f32[4,112]{1,0:T(4,128)}, u32[]{:S(2)}) copy-start(f32[4,112]{1,0:T(4,128)} %param.35) | copy-start | bytes 5380
  410.6 14.9 %collective-permute-start.2 = (f32[8,448]{1,0:T(8,128)S(1)}, f32[8,448]{1,0:T(8,128)S(1)}, u32[]{:S(2)}, u32[]{:S(2)}) collective-permute-start(f32[8,448]{1,0:T(8,128)S(1)} %fusion.1), channel_id=1, source_target_pairs={{0,1},{1,2},{2,3},{3,32},{32,33},{33,34},{34,35},{35,64},{64,65},{... | collective-permute-start | bytes 43016
  412.5 19.8 %collective-permute-start.3 = (f32[8,448]{1,0:T(8,128)S(1)}, f32[8,448]{1,0:T(8,128)S(1)}, u32[]{:S(2)}, u32[]{:S(2)}) collective-permute-start(f32[8,448]{1,0:T(8,128)S(1)} %fusion.1), channel_id=1, source_target_pairs={{0,2},{1,3},{2,32},{3,33},{32,34},{33,35},{34,64},{35,65},{64,66},... | collective-permute-start | bytes 43016
  414.5 5.2 collective-permute-start.9
  415.8 21.8 %collective-permute-start.4 = (f32[8,448]{1,0:T(8,128)S(1)}, f32[8,448]{1,0:T(8,128)S(1)}, u32[]{:S(2)}, u32[]{:S(2)}) collective-permute-start(f32[8,448]{1,0:T(8,128)S(1)} %fusion.1), channel_id=1, source_target_pairs={{0,3},{1,32},{2,33},{3,34},{32,35},{33,64},{34,65},{35,66},{64,67}... | collective-permute-start | bytes 43016
  417.7 19.9 %collective-permute-start.5 = (f32[8,448]{1,0:T(8,128)S(1)}, f32[8,448]{1,0:T(8,128)S(1)}, u32[]{:S(2)}, u32[]{:S(2)}) collective-permute-start(f32[8,448]{1,0:T(8,128)S(1)} %fusion.1), channel_id=1, source_target_pairs={{0,32},{1,33},{2,34},{3,35},{32,64},{33,65},{34,66},{35,67},{64,96... | collective-permute-start | bytes 43016
  419.6 17.9 %collective-permute-start.6 = (f32[8,448]{1,0:T(8,128)S(1)}, f32[8,448]{1,0:T(8,128)S(1)}, u32[]{:S(2)}, u32[]{:S(2)}) collective-permute-start(f32[8,448]{1,0:T(8,128)S(1)} %fusion.1), channel_id=1, source_target_pairs={{0,33},{1,34},{2,35},{3,64},{32,65},{33,66},{34,67},{35,96},{64,97... | collective-permute-start | bytes 43016
  425.5 12.1 %collective-permute-start.7 = (f32[8,448]{1,0:T(8,128)S(1)}, f32[8,448]{1,0:T(8,128)S(1)}, u32[]{:S(2)}, u32[]{:S(2)}) collective-permute-start(f32[8,448]{1,0:T(8,128)S(1)} %fusion.1), channel_id=1, source_target_pairs={{0,34},{1,35},{2,64},{3,65},{32,66},{33,67},{34,96},{35,97},{64,98... | collective-permute-start | bytes 43016
  432.4 5.2 collective-permute-start.8
  437.5 141.7 %copy-start.5 = (s32[5,48,4,8]{1,3,2,0:T(8,128)S(1)}, s32[5,48,4,8]{1,3,2,0:T(8,128)}, u32[]{:S(2)}) copy-start(s32[5,48,4,8]{1,3,2,0:T(8,128)} %param.37) | copy-start | bytes 92164
  512.1 106.0 %all-gather.12.cloned.1.call-start = ((), (), s32[]{:S(2)}) async-start(), calls=%async_computation.5 | async-start | bytes 1769472 | tf_op jit(solution)/shard_map/all_gather | solution.py:168
  513.0 67.6 %copy-start.21 = (s32[1,5]{1,0:T(1,128)S(1)}, s32[1,5]{1,0:T(1,128)}, u32[]{:S(2)}) copy-start(s32[1,5]{1,0:T(1,128)} %param.31) | copy-start | bytes 64
  513.0 166.3 %all-gather.10.cloned.1.call-start = ((), (), s32[]{:S(2)}) async-start(), calls=%async_computation.4 | async-start | bytes 7569408 | tf_op jit(solution)/shard_map/all_gather | solution.py:176
  626.9 60.7 %copy-start.6 = (s32[192,5]{0,1:T(8,128)S(1)}, s32[192,5]{0,1:T(8,128)}, u32[]{:S(2)}) copy-start(s32[192,5]{0,1:T(8,128)} %get-tuple-element.43) | copy-start | bytes 11524
  626.9 60.7 %copy-start.7 = (s32[192,5]{0,1:T(8,128)S(1)}, s32[192,5]{0,1:T(8,128)}, u32[]{:S(2)}) copy-start(s32[192,5]{0,1:T(8,128)} %get-tuple-element.44) | copy-start | bytes 11524
  626.9 60.7 %copy-start.8 = (s32[192,5]{0,1:T(8,128)S(1)}, s32[192,5]{0,1:T(8,128)}, u32[]{:S(2)}) copy-start(s32[192,5]{0,1:T(8,128)} %get-tuple-element.45) | copy-start | bytes 11524
  626.9 60.7 %copy-start.9 = (s32[192,5]{0,1:T(8,128)S(1)}, s32[192,5]{0,1:T(8,128)}, u32[]{:S(2)}) copy-start(s32[192,5]{0,1:T(8,128)} %get-tuple-element.46) | copy-start | bytes 11524
  626.9 60.7 %copy-start.10 = (s32[192,5]{0,1:T(8,128)S(1)}, s32[192,5]{0,1:T(8,128)}, u32[]{:S(2)}) copy-start(s32[192,5]{0,1:T(8,128)} %get-tuple-element.47) | copy-start | bytes 11524
  626.9 60.7 %copy-start.11 = (s32[192,5]{0,1:T(8,128)S(1)}, s32[192,5]{0,1:T(8,128)}, u32[]{:S(2)}) copy-start(s32[192,5]{0,1:T(8,128)} %get-tuple-element.48) | copy-start | bytes 11524
  626.9 60.7 %copy-start.12 = (s32[192,5]{0,1:T(8,128)S(1)}, s32[192,5]{0,1:T(8,128)}, u32[]{:S(2)}) copy-start(s32[192,5]{0,1:T(8,128)} %get-tuple-element.49) | copy-start | bytes 11524
Sparse Core Ops, SparseCore 0:
  26.3 68.1 all-reduce.12
  111.9 73.9 all-reduce.14
  272.3 68.5 all-reduce.16
  512.2 65.0 all-reduce.18
  578.9 39.1 all-gather.11
  620.5 58.7 all-gather.9
